TPU v7x, 256 devices: a whole 4x4x8 slice. The times are simulated.
256 devices in a mesh: probe: 4 (over y_lo, core), tile: 32 (over z, x), level: 2 (over y_hi).
Axes of the slice: x: 4, y: 4 (y_hi: 2, y_lo: 2; y = y_hi * 2 + y_lo), z: 8, core: 2. Of those that a mesh axis runs over, the one named last changes fastest.
Arguments:
- probe_bits: int32 [4, 64, 256, 256], P('probe', 'level', 'tile'), may hold values from 0 to 1
- kappa_sq: float32 [64, 256, 256], P('level', 'tile'), may hold values from 0.25 to 4
- observed: float32 [64, 256, 256], P('level', 'tile'), may hold values from -0.6 to 0.6
Outputs:
- gradient: float32 [64, 256, 256], P('level', 'tile', 'probe')
Inputs may be any that keep to these rules, and one draw needn't show every extreme that they name: `probe_bits`: a probe's sign is 2 times its bit minus 1.
All inputs are finite; a program needn't handle non-finite values.
Results may differ from a plain program's by a relative error of at most 0.0003.
Values sent between devices are 32-bit elements; how exact they have to be, the bound alone decides.
A program may use at most 64 MiB of HBM per device.

v0:
```python
import jax
import jax.numpy as jnp
from jax import lax
from jax.sharding import PartitionSpec as P

ITERS = 4
VERTICAL = 2.0


def with_halo(cells, sides, width):
    for axis, dim in sides:
        count = lax.axis_size(axis)
        ends = count - 1
        head = lax.slice_in_dim(cells, 0, width, axis=dim)
        tail = lax.slice_in_dim(cells, cells.shape[dim] - width, cells.shape[dim], axis=dim)
        cells = jnp.concatenate(
            [
                lax.ppermute(tail, axis, [(i, (i + 1) % count) for i in range(ends)]),
                cells,
                lax.ppermute(head, axis, [((i + 1) % count, i) for i in range(ends)]),
            ],
            axis=dim,
        )
    return cells


def shift_levels(values, stride, level_dim, fill_value):
    level_count = values.shape[level_dim]
    widths = [(0, 0)] * values.ndim
    if stride > 0:
        widths[level_dim] = (stride, 0)
        padded = jnp.pad(values, widths, constant_values=fill_value)
        return lax.slice_in_dim(padded, 0, level_count, axis=level_dim)
    widths[level_dim] = (0, -stride)
    padded = jnp.pad(values, widths, constant_values=fill_value)
    return lax.slice_in_dim(padded, -stride, level_count - stride, axis=level_dim)


def reduction_tables(kappa_sq):
    level_count = kappa_sq.shape[0]
    level_ids = lax.broadcasted_iota(jnp.int32, kappa_sq.shape, 0)
    diagonal = kappa_sq + (4.0 + 2.0 * VERTICAL)
    lower = jnp.where(level_ids > 0, -VERTICAL, 0.0).astype(jnp.float32)
    upper = jnp.where(level_ids < level_count - 1, -VERTICAL, 0.0).astype(jnp.float32)
    tables = []
    stride = 1
    while stride < level_count:
        lower_ratio = -lower / shift_levels(diagonal, stride, 0, 1.0)
        upper_ratio = -upper / shift_levels(diagonal, -stride, 0, 1.0)
        new_diagonal = (
            diagonal
            + lower_ratio * shift_levels(upper, stride, 0, 0.0)
            + upper_ratio * shift_levels(lower, -stride, 0, 0.0)
        )
        new_lower = lower_ratio * shift_levels(lower, stride, 0, 0.0)
        upper = upper_ratio * shift_levels(upper, -stride, 0, 0.0)
        lower = new_lower
        diagonal = new_diagonal
        tables.append((lower_ratio, upper_ratio, stride))
        stride = stride * 2
    return (tables, 1.0 / diagonal)


def vertical_solve(values, tables, inverse_diagonal):
    for lower_ratio, upper_ratio, stride in tables:
        values = (
            values
            + lower_ratio * shift_levels(values, stride, 1, 0.0)
            + upper_ratio * shift_levels(values, -stride, 1, 0.0)
        )
    return values * inverse_diagonal


def stencil(padded, values, kappa_sq):
    beside_x = padded[:, 1:-1, 2:, 1:-1] + padded[:, 1:-1, :-2, 1:-1]
    beside_y = padded[:, 1:-1, 1:-1, 2:] + padded[:, 1:-1, 1:-1, :-2]
    beside_z = padded[:, 2:, 1:-1, 1:-1] + padded[:, :-2, 1:-1, 1:-1]
    return (kappa_sq + (4.0 + 2.0 * VERTICAL)) * values - beside_x - beside_y - VERTICAL * beside_z


def slab_apply(values, kappa_sq):
    extended = with_halo(values, (("tile", 2), ("level", 1)), 1)
    padded = jnp.pad(extended, ((0, 0), (0, 0), (0, 0), (1, 1)))
    return stencil(padded, values, kappa_sq)


def local_dots(first, second):
    return jnp.sum(first * second, axis=(1, 2, 3))


def precond_total(residual, precond):
    return lax.psum(local_dots(residual, precond), ("tile", "level"))


def conjugate_solve(right_side, apply_q, apply_m):
    shaped = (right_side.shape[0], 1, 1, 1)
    solution = jnp.zeros_like(right_side)
    residual = right_side
    precond = apply_m(residual)
    rho_now = precond_total(residual, precond)
    direction = precond
    for iteration in range(ITERS):
        image_field = apply_q(direction)
        curv_total = lax.psum(local_dots(direction, image_field), ("tile", "level"))
        step_size = (rho_now / curv_total).reshape(shaped)
        solution = solution + step_size * direction
        if iteration + 1 < ITERS:
            residual = residual - step_size * image_field
            precond = apply_m(residual)
            rho_next = precond_total(residual, precond)
            direction = precond + (rho_next / rho_now).reshape(shaped) * direction
            rho_now = rho_next
    return solution


def body(probe_bits, kappa_sq, observed):
    sign_field = (2 * probe_bits - 1).astype(jnp.float32)
    stacked = jnp.concatenate([sign_field, observed[None]], axis=0)
    extended = with_halo(stacked, (("tile", 2), ("level", 1)), 1)
    padded = jnp.pad(extended, ((0, 0), (0, 0), (0, 0), (1, 1)))
    k_stacked = stencil(padded, stacked, kappa_sq)
    k_signs = k_stacked[:-1]
    data_term = 2.0 * observed * k_stacked[-1]
    kappa_cols = lax.all_to_all(kappa_sq[None], "level", split_axis=3, concat_axis=1, tiled=True)[0]
    tables, inverse_diagonal = reduction_tables(kappa_cols)

    def solve_columns(columns):
        solved = vertical_solve(
            vertical_solve(columns, tables, inverse_diagonal), tables, inverse_diagonal
        )
        return lax.all_to_all(solved, "level", split_axis=1, concat_axis=3, tiled=True)

    def apply_m(values):
        return solve_columns(
            lax.all_to_all(values, "level", split_axis=3, concat_axis=1, tiled=True)
        )

    def apply_q(values):
        return slab_apply(slab_apply(values, kappa_sq), kappa_sq)

    solution = conjugate_solve(sign_field, apply_q, apply_m)
    probe_partial = jnp.sum(
        solution * k_signs + slab_apply(solution, kappa_sq) * sign_field, axis=0
    )
    summed = lax.psum_scatter(probe_partial, "probe", scatter_dimension=2, tiled=True)
    y_width = summed.shape[2]
    offset = lax.axis_index("probe") * y_width
    kappa_part = lax.dynamic_slice_in_dim(kappa_sq, offset, y_width, 2)
    data_part = lax.dynamic_slice_in_dim(data_term, offset, y_width, 2)
    probe_count = probe_bits.shape[0] * lax.axis_size("probe")
    return kappa_part * (summed / probe_count - data_part)


def solution(mesh):
    in_specs = (
        P("probe", "level", "tile", None),
        P("level", "tile", None),
        P("level", "tile", None),
    )
    out_specs = P("level", "tile", "probe")
    return jax.shard_map(body, mesh=mesh, in_specs=in_specs, out_specs=out_specs, check_vma=False)
```

profile of v0, /device:TPU:1, one launch (start us, length us, event | category | flops | bytes accessed | tf_op | source)
XLA Modules:
  0.0 1670.7 jit_solution(17637381411247329690)
XLA Ops:
  9.1 5.0 all-to-all-start.1
  15.8 3.9 all-to-all-done.1
  19.7 3.4 all-to-all-start
  26.1 2.6 all-to-all-done
  33.5 8.0 all_to_all.165
  43.0 4.0 collective-permute-start.1
  51.2 4.7 collective-permute-done.3
  58.1 4.3 collective-permute-start.5
  66.3 4.7 collective-permute-done.7
  73.2 158.1 %all-reduce.140 = (f32[1]{0:T(128)}, f32[1]{0:T(128)}) all-reduce(f32[1]{0:T(128)} %bitcast.26, f32[1]{0:T(128)} %bitcast.30), channel_id=1, replica_groups=mesh['probe'=4,'tile'=32,'level'=2] {'tile','level'}, use_global_device_ids=true, to_apply=%region_1.2 | all-reduce | flops 2 | bytes 16 | tf_op jit(solution)/shard_map/psum | solution.py:92
  239.0 9.9 all_to_all.166
  249.0 3.1 reduce.10
  252.0 2.4 reshape.184
  259.4 8.0 all_to_all.167
  268.1 149.1 %psum.58 = f32[1]{0:T(128)} all-reduce(f32[1]{0:T(128)} %bitcast.39), channel_id=1, replica_groups=mesh['probe'=4,'tile'=32,'level'=2] {'tile','level'}, use_global_device_ids=true, to_apply=%region_5.6 | all-reduce | flops 1 | bytes 8 | tf_op jit(solution)/shard_map/psum | solution.py:92
  420.8 4.0 collective-permute-start.9
  425.9 5.0 collective-permute-start.10
  432.2 5.0 collective-permute-done.11
  440.1 4.0 collective-permute-start.13
  448.0 4.7 collective-permute-done.15
  454.8 149.1 %psum.59 = f32[1]{0:T(128)} all-reduce(f32[1]{0:T(128)} %bitcast.43), channel_id=1, replica_groups=mesh['probe'=4,'tile'=32,'level'=2] {'tile','level'}, use_global_device_ids=true, to_apply=%region_7.8 | all-reduce | flops 1 | bytes 8 | tf_op jit(solution)/shard_map/psum | solution.py:104
  611.7 10.3 all_to_all.168
  622.0 3.1 reduce.11
  625.1 2.4 reshape.186
  632.5 7.9 all_to_all.169
  641.7 149.8 %psum.60 = f32[1]{0:T(128)} all-reduce(f32[1]{0:T(128)} %bitcast.52), channel_id=1, replica_groups=mesh['probe'=4,'tile'=32,'level'=2] {'tile','level'}, use_global_device_ids=true, to_apply=%region_9.10 | all-reduce | flops 1 | bytes 8 | tf_op jit(solution)/shard_map/psum | solution.py:92
  795.2 4.0 collective-permute-start.17
  800.2 4.4 collective-permute-start.18
  805.9 4.7 collective-permute-done.19
  812.8 4.3 collective-permute-start.21
  821.1 5.0 collective-permute-done.23
  828.2 149.4 %psum.61 = f32[1]{0:T(128)} all-reduce(f32[1]{0:T(128)} %bitcast.56), channel_id=1, replica_groups=mesh['probe'=4,'tile'=32,'level'=2] {'tile','level'}, use_global_device_ids=true, to_apply=%region_11.12 | all-reduce | flops 1 | bytes 8 | tf_op jit(solution)/shard_map/psum | solution.py:104
  985.3 10.2 all_to_all.170
  995.5 3.1 reduce.12
  1006.0 8.1 all_to_all.171
  1014.8 150.4 %psum.62 = f32[1]{0:T(128)} all-reduce(f32[1]{0:T(128)} %bitcast.65), channel_id=1, replica_groups=mesh['probe'=4,'tile'=32,'level'=2] {'tile','level'}, use_global_device_ids=true, to_apply=%region_13.14 | all-reduce | flops 1 | bytes 8 | tf_op jit(solution)/shard_map/psum | solution.py:92
  1167.8 4.0 collective-permute-start.25
  1172.9 4.1 collective-permute-start.26
  1179.7 4.3 collective-permute-start.33
  1186.2 4.0 collective-permute-start.29
  1191.2 5.6 collective-permute-start.30
  1198.2 5.5 collective-permute-start.34
  1206.5 152.8 %psum.63 = f32[1]{0:T(128)} all-reduce(f32[1]{0:T(128)} %bitcast.69), channel_id=1, replica_groups=mesh['probe'=4,'tile'=32,'level'=2] {'tile','level'}, use_global_device_ids=true, to_apply=%region_15.16 | all-reduce | flops 1 | bytes 8 | tf_op jit(solution)/shard_map/psum | solution.py:104
  1362.0 4.0 collective-permute-start.37
  1371.2 3.9 collective-permute-done.39
  1376.1 4.4 copy.71
  1380.5 4.7 reshape.177
  1385.2 275.9 %reduce-scatter.4.cloned.1.call-done = f32[64,256]{1,0:T(8,128)} async-done(((f32[256,256]{1,0:T(8,128)}), f32[64,256]{1,0:T(8,128)}) %reduce-scatter.4.cloned.1.call-update) | async-done | bytes 65552
  (253 shorter events, 113.9 us)
Async XLA Ops:
  9.1 10.5 all-to-all-start.1
  19.7 9.0 all-to-all-start
  23.1 1637.9 %reduce-scatter.4.cloned.1.call-start = ((), (), s32[]{:S(2)}) async-start(), calls=%async_computation.10 | async-start | bytes 327680
  41.7 5.3 collective-permute-start
  43.0 5.0 collective-permute-start.1
  48.0 3.2 collective-permute-start.2
  49.9 6.0 collective-permute-start.3
  56.8 5.6 collective-permute-start.4
  58.1 5.3 collective-permute-start.5
  63.4 3.0 collective-permute-start.6
  65.0 6.0 collective-permute-start.7
  419.5 5.3 collective-permute-start.8
  420.8 5.0 collective-permute-start.9
  425.9 6.3 collective-permute-start.10
  430.9 6.3 collective-permute-start.11
  438.8 5.3 collective-permute-start.12
  440.1 5.0 collective-permute-start.13
  445.1 2.9 collective-permute-start.14
  446.7 6.0 collective-permute-start.15
  793.9 5.3 collective-permute-start.16
  795.2 5.0 collective-permute-start.17
  800.2 5.7 collective-permute-start.18
  804.6 6.0 collective-permute-start.19
  811.5 5.6 collective-permute-start.20
  812.8 5.3 collective-permute-start.21
  818.1 3.0 collective-permute-start.22
  819.7 6.3 collective-permute-start.23
  1005.9 172.4 %copy-start.10 = (f32[1,32,8,256]{3,2,1,0:T(8,128)S(1)}, f32[1,32,8,256]{3,2,1,0:T(8,128)}, u32[]{:S(2)}) copy-start(f32[1,32,8,256]{3,2,1,0:T(8,128)} %copy-done.9) | copy-start | bytes 786436
  1005.9 172.4 %copy-start.14 = (f32[32,8,256]{2,1,0:T(8,128)S(1)}, f32[32,8,256]{2,1,0:T(8,128)}, u32[]{:S(2)}) copy-start(f32[32,8,256]{2,1,0:T(8,128)} %param.5) | copy-start | bytes 786436
  1014.8 169.8 %copy-start.13 = (f32[1,64,8,128]{3,2,0,1:T(8,128)S(1)}, f32[1,64,8,128]{3,2,0,1:T(8,128)}, u32[]{:S(2)}) copy-start(f32[1,64,8,128]{3,2,0,1:T(8,128)} %copy-done.11) | copy-start | bytes 786436
  1014.8 169.8 %copy-start.23 = (f32[32,8,256]{2,1,0:T(8,128)S(1)}, f32[32,8,256]{2,1,0:T(8,128)}, u32[]{:S(2)}) copy-start(f32[32,8,256]{2,1,0:T(8,128)} %get-tuple-element.14) | copy-start | bytes 786436
  1166.5 5.3 collective-permute-start.24
  1167.8 5.0 collective-permute-start.25
  1172.9 11.1 collective-permute-start.26
  1177.0 7.0 collective-permute-start.27
  1178.4 19.8 %collective-permute-start.32 = (f32[2,32,1,256]{3,2,1,0:T(1,128)S(1)}, f32[2,32,1,256]{3,2,1,0:T(1,128)S(1)}, u32[]{:S(2)}, u32[]{:S(2)}) collective-permute-start(f32[2,32,1,256]{3,2,1,0:T(1,128)S(1)} %get-tuple-element.47), channel_id=1, source_target_pairs={{2,0},{4,2},{6,4},{8,6},{10,8},{12,10},{14,12},{16,14},{18,16},{20... | collective-permute-start | bytes 196616 | tf_op jit(solution)/shard_map/ppermute | solution.py:20
  1179.7 18.5 %collective-permute-start.33 = (f32[2,32,1,256]{3,2,1,0:T(1,128)S(1)}, f32[2,32,1,256]{3,2,1,0:T(1,128)S(1)}, u32[]{:S(2)}, u32[]{:S(2)}) collective-permute-start(f32[2,32,1,256]{3,2,1,0:T(1,128)S(1)} %get-tuple-element.46), channel_id=1, source_target_pairs={{0,2},{2,4},{4,6},{6,8},{8,10},{10,12},{12,14},{14,16},{16,18},{18... | collective-permute-start | bytes 196616 | tf_op jit(solution)/shard_map/ppermute | solution.py:18
  1184.9 5.3 collective-permute-start.28
  1186.2 5.0 collective-permute-start.29
  1191.2 169.4 %copy-start.6 = (f32[1,32,8,256]{3,2,1,0:T(8,128)S(1)}, f32[1,32,8,256]{3,2,1,0:T(8,128)}, u32[]{:S(2)}) copy-start(f32[1,32,8,256]{3,2,1,0:T(8,128)} %copy-done.5) | copy-start | bytes 786436
  1191.2 13.8 collective-permute-start.30
  1196.9 8.2 collective-permute-start.31
  1198.2 167.8 %collective-permute-start.34 = (f32[2,1,10,256]{3,2,1,0:T(8,128)S(1)}, f32[2,1,10,256]{3,2,1,0:T(8,128)S(1)}, u32[]{:S(2)}, u32[]{:S(2)}) collective-permute-start(f32[2,1,10,256]{3,2,1,0:T(8,128)S(1)} %get-tuple-element.39), channel_id=1, source_target_pairs={{0,1},{2,3},{4,5},{6,7},{8,9},{10,11},{12,13},{14,15},{16,17},{18,... | collective-permute-start | bytes 61448 | tf_op jit(solution)/shard_map/ppermute | solution.py:18
  1203.7 162.3 %collective-permute-start.35 = (f32[2,1,10,256]{3,2,1,0:T(8,128)S(1)}, f32[2,1,10,256]{3,2,1,0:T(8,128)S(1)}, u32[]{:S(2)}, u32[]{:S(2)}) collective-permute-start(f32[2,1,10,256]{3,2,1,0:T(8,128)S(1)} %get-tuple-element.38), channel_id=1, source_target_pairs={{1,0},{3,2},{5,4},{7,6},{9,8},{11,10},{13,12},{15,14},{17,16},{19,... | collective-permute-start | bytes 61448 | tf_op jit(solution)/shard_map/ppermute | solution.py:20
  1360.7 6.3 collective-permute-start.36
  1362.0 5.0 collective-permute-start.37
  1367.1 4.1 collective-permute-start.38
  1369.0 6.1 collective-permute-start.39
  (20 other events, 378.9 us)
Sparse Core Ops, SparseCore 0:
  1385.3 275.7 reduce-scatter.3
where the time goes:
time: 1670 us
  blocking collectives  1120 us (67%)
  waiting for transfers between devices  323 us (19%)
  starting transfers between devices  109 us (7%)
  local copies, waits for them, and re-layouts  52.3 us (3%)
  other arithmetic  41.6 us (2%)
  between operations  23.8 us (1%)
    psum x4, blocking collectives, precond_total(): return lax.psum(local_dots(residual, precond), ('tile', 'level'))  607 us
    psum x3, blocking collectives, conjugate_solve(): curv_total = lax.psum(local_dots(direction, image_field), ('tile', 'level'))  451 us
    unnamed x2, waiting for transfers between devices  276 us
    ppermute x20, starting transfers between devices, with_halo(): lax.ppermute(tail, axis, [(i, (i + 1) % count) for i in range(ends)])  74.2 us
  transfers between devices with their start and end apart: 43, of which 18 were waited for; matrix products, arithmetic and copies ran while one was open for 1% of the time, Pallas kernels for 0%

commit v1 on v0

--- a/solution.py
+++ b/solution.py
@@ -5,6 +5,11 @@
 
 ITERS = 4
 VERTICAL = 2.0
+
+
+def axis_by_axis(array, leading, second_2):
+    inner = lax.psum(array, leading)
+    return lax.psum(inner, second_2)
 
 
 def with_halo(cells, sides, width):
@@ -89,7 +94,7 @@
 
 
 def precond_total(residual, precond):
-    return lax.psum(local_dots(residual, precond), ("tile", "level"))
+    return axis_by_axis(local_dots(residual, precond), "level", "tile")
 
 
 def conjugate_solve(right_side, apply_q, apply_m):

time: 1670 us -> 1460 us (0.87)
  blocking collectives: 1120 us -> 937 us
  waiting for transfers between devices: 323 us -> 287 us
    psum x4 -> x8, blocking collectives: 607 us -> 260 us  [the longest x4 236 us: axis_by_axis(): return lax.psum(inner, second_2)]
    psum x3 -> x4, blocking collectives: 451 us -> 615 us  [conjugate_solve(): curv_total = lax.psum(local_dots(direction, image_field), ('tile', 'level'))]
    unnamed x2, waiting for transfers between devices: 276 us -> 242 us
where the time goes in v1:
time: 1460 us; the launch traced here: 1450 us
  blocking collectives  937 us (64%)
  waiting for transfers between devices  287 us (20%)
  starting transfers between devices  101 us (7%)
  local copies, waits for them, and re-layouts  52.3 us (4%)
  other arithmetic  43.2 us (3%)
  between operations  24.5 us (2%)
    psum x4, blocking collectives, conjugate_solve(): curv_total = lax.psum(local_dots(direction, image_field), ('tile', 'level'))  615 us
    unnamed x2, waiting for transfers between devices  242 us
    psum x4, blocking collectives, axis_by_axis(): return lax.psum(inner, second_2)  236 us
    ppermute x20, starting transfers between devices, with_halo(): lax.ppermute(tail, axis, [(i, (i + 1) % count) for i in range(ends)])  65.9 us
    unnamed x72, local copies, waits for them, and re-layouts  33.4 us
    all_to_all x4, blocking collectives, solve_columns(): lax.all_to_all(solved, 'level', split_axis=1, concat_axis=3, tiled=True)  32.7 us
    ppermute x20, waiting for transfers between devices, with_halo(): lax.ppermute(head, axis, [((i + 1) % count, i) for i in range(ends)])  31.3 us
    all_to_all x3, blocking collectives, apply_m(): lax.all_to_all(values, 'level', split_axis=3, concat_axis=1, tiled=True)  29.9 us
  transfers between devices with their start and end apart: 43, of which 18 were waited for; matrix products, arithmetic and copies ran while one was open for 1% of the time, Pallas kernels for 0%

profile of v1, /device:TPU:1, one launch (start us, length us, event | category | flops | bytes accessed | tf_op | source)
XLA Modules:
  0.0 1445.1 jit_solution(16941950590230095580)
XLA Ops:
  9.2 5.0 all-to-all-start.1
  15.8 3.9 all-to-all-done.1
  19.7 3.4 all-to-all-start
  26.1 2.6 all-to-all-done
  33.5 8.0 all_to_all.165
  42.9 4.0 collective-permute-start.1
  51.2 4.7 collective-permute-done.3
  58.0 4.3 collective-permute-start.5
  66.3 4.7 collective-permute-done.7
  73.2 5.9 psum.84
  79.1 65.5 %psum.85 = f32[1]{0:T(128)} all-reduce(f32[1]{0:T(128)} %psum.84), channel_id=1, replica_groups=mesh['probe'=4,'tile'=32,'level'=2] {'tile'}, use_global_device_ids=true, to_apply=%region_2.3 | all-reduce | flops 1 | bytes 8 | tf_op jit(solution)/shard_map/psum | solution.py:12
  144.6 150.1 %psum.86 = f32[1]{0:T(128)} all-reduce(f32[1]{0:T(128)} %bitcast.30), channel_id=1, replica_groups=mesh['probe'=4,'tile'=32,'level'=2] {'tile','level'}, use_global_device_ids=true, to_apply=%region_4.5 | all-reduce | flops 1 | bytes 8 | tf_op jit(solution)/shard_map/psum | solution.py:109
  302.3 10.2 all_to_all.166
  312.6 3.1 reduce.10
  323.0 8.3 all_to_all.167
  332.1 6.0 psum.87
  338.0 56.3 %psum.88 = f32[1]{0:T(128)} all-reduce(f32[1]{0:T(128)} %psum.87), channel_id=1, replica_groups=mesh['probe'=4,'tile'=32,'level'=2] {'tile'}, use_global_device_ids=true, to_apply=%region_7.8 | all-reduce | flops 1 | bytes 8 | tf_op jit(solution)/shard_map/psum | solution.py:12
  398.0 4.1 collective-permute-start.9
  406.5 4.7 collective-permute-done.11
  414.1 4.3 collective-permute-start.13
  422.3 4.7 collective-permute-done.15
  429.2 150.2 %psum.89 = f32[1]{0:T(128)} all-reduce(f32[1]{0:T(128)} %bitcast.43), channel_id=1, replica_groups=mesh['probe'=4,'tile'=32,'level'=2] {'tile','level'}, use_global_device_ids=true, to_apply=%region_9.10 | all-reduce | flops 1 | bytes 8 | tf_op jit(solution)/shard_map/psum | solution.py:109
  587.1 9.8 all_to_all.168
  596.9 3.1 reduce.11
  607.4 8.0 all_to_all.169
  616.8 6.3 psum.90
  623.1 57.0 %psum.91 = f32[1]{0:T(128)} all-reduce(f32[1]{0:T(128)} %psum.90), channel_id=1, replica_groups=mesh['probe'=4,'tile'=32,'level'=2] {'tile'}, use_global_device_ids=true, to_apply=%region_12.13 | all-reduce | flops 1 | bytes 8 | tf_op jit(solution)/shard_map/psum | solution.py:12
  683.9 4.2 collective-permute-start.17
  692.0 4.7 collective-permute-done.19
  698.9 4.3 collective-permute-start.21
  707.2 4.7 collective-permute-done.23
  714.0 151.3 %psum.92 = f32[1]{0:T(128)} all-reduce(f32[1]{0:T(128)} %bitcast.56), channel_id=1, replica_groups=mesh['probe'=4,'tile'=32,'level'=2] {'tile','level'}, use_global_device_ids=true, to_apply=%region_14.15 | all-reduce | flops 1 | bytes 8 | tf_op jit(solution)/shard_map/psum | solution.py:109
  873.1 9.9 all_to_all.170
  883.1 3.1 reduce.12
  893.5 8.4 all_to_all.171
  902.6 5.9 psum.93
  908.5 57.2 %psum.94 = f32[1]{0:T(128)} all-reduce(f32[1]{0:T(128)} %psum.93), channel_id=1, replica_groups=mesh['probe'=4,'tile'=32,'level'=2] {'tile'}, use_global_device_ids=true, to_apply=%region_17.18 | all-reduce | flops 1 | bytes 8 | tf_op jit(solution)/shard_map/psum | solution.py:12
  968.5 4.0 collective-permute-start.25
  977.8 4.3 collective-permute-start.33
  984.3 4.0 collective-permute-start.29
  989.3 5.6 collective-permute-start.30
  996.3 5.5 collective-permute-start.34
  1004.6 162.9 %psum.95 = f32[1]{0:T(128)} all-reduce(f32[1]{0:T(128)} %bitcast.69), channel_id=1, replica_groups=mesh['probe'=4,'tile'=32,'level'=2] {'tile','level'}, use_global_device_ids=true, to_apply=%region_19.20 | all-reduce | flops 1 | bytes 8 | tf_op jit(solution)/shard_map/psum | solution.py:109
  1170.4 4.0 collective-permute-start.37
  1179.8 3.2 collective-permute-done.39
  1183.9 4.3 copy.71
  1188.3 4.7 reshape.177
  1193.0 242.2 %reduce-scatter.4.cloned.1.call-done = f32[64,256]{1,0:T(8,128)} async-done(((f32[256,256]{1,0:T(8,128)}), f32[64,256]{1,0:T(8,128)}) %reduce-scatter.4.cloned.1.call-update) | async-done | bytes 65552
  (264 shorter events, 124.4 us)
Async XLA Ops:
  9.2 10.5 all-to-all-start.1
  19.7 9.0 all-to-all-start
  23.1 1412.1 %reduce-scatter.4.cloned.1.call-start = ((), (), s32[]{:S(2)}) async-start(), calls=%async_computation.10 | async-start | bytes 327680
  41.6 5.3 collective-permute-start
  42.9 5.0 collective-permute-start.1
  47.9 3.2 collective-permute-start.2
  49.8 6.0 collective-permute-start.3
  56.7 5.6 collective-permute-start.4
  58.0 5.3 collective-permute-start.5
  63.3 3.0 collective-permute-start.6
  65.0 6.0 collective-permute-start.7
  396.7 5.4 collective-permute-start.8
  398.0 5.1 collective-permute-start.9
  403.2 3.4 collective-permute-start.10
  405.2 6.0 collective-permute-start.11
  412.8 5.6 collective-permute-start.12
  414.1 5.3 collective-permute-start.13
  419.4 3.0 collective-permute-start.14
  421.0 6.0 collective-permute-start.15
  682.6 5.5 collective-permute-start.16
  683.9 5.2 collective-permute-start.17
  689.1 2.9 collective-permute-start.18
  690.7 6.0 collective-permute-start.19
  697.6 5.6 collective-permute-start.20
  698.9 5.3 collective-permute-start.21
  704.2 3.0 collective-permute-start.22
  705.9 6.0 collective-permute-start.23
  893.4 82.9 %copy-start.10 = (f32[1,32,8,256]{3,2,1,0:T(8,128)S(1)}, f32[1,32,8,256]{3,2,1,0:T(8,128)}, u32[]{:S(2)}) copy-start(f32[1,32,8,256]{3,2,1,0:T(8,128)} %copy-done.9) | copy-start | bytes 786436
  893.5 82.9 %copy-start.14 = (f32[32,8,256]{2,1,0:T(8,128)S(1)}, f32[32,8,256]{2,1,0:T(8,128)}, u32[]{:S(2)}) copy-start(f32[32,8,256]{2,1,0:T(8,128)} %param.5) | copy-start | bytes 786436
  902.6 80.0 %copy-start.13 = (f32[1,64,8,128]{3,2,0,1:T(8,128)S(1)}, f32[1,64,8,128]{3,2,0,1:T(8,128)}, u32[]{:S(2)}) copy-start(f32[1,64,8,128]{3,2,0,1:T(8,128)} %copy-done.11) | copy-start | bytes 786436
  902.6 80.1 %copy-start.23 = (f32[32,8,256]{2,1,0:T(8,128)S(1)}, f32[32,8,256]{2,1,0:T(8,128)}, u32[]{:S(2)}) copy-start(f32[32,8,256]{2,1,0:T(8,128)} %get-tuple-element.12) | copy-start | bytes 786436
  967.2 5.3 collective-permute-start.24
  968.5 5.0 collective-permute-start.25
  973.5 8.6 collective-permute-start.26
  975.1 7.0 collective-permute-start.27
  976.5 19.8 %collective-permute-start.32 = (f32[2,32,1,256]{3,2,1,0:T(1,128)S(1)}, f32[2,32,1,256]{3,2,1,0:T(1,128)S(1)}, u32[]{:S(2)}, u32[]{:S(2)}) collective-permute-start(f32[2,32,1,256]{3,2,1,0:T(1,128)S(1)} %get-tuple-element.45), channel_id=1, source_target_pairs={{2,0},{4,2},{6,4},{8,6},{10,8},{12,10},{14,12},{16,14},{18,16},{20... | collective-permute-start | bytes 196616 | tf_op jit(solution)/shard_map/ppermute | solution.py:25
  977.8 18.5 %collective-permute-start.33 = (f32[2,32,1,256]{3,2,1,0:T(1,128)S(1)}, f32[2,32,1,256]{3,2,1,0:T(1,128)S(1)}, u32[]{:S(2)}, u32[]{:S(2)}) collective-permute-start(f32[2,32,1,256]{3,2,1,0:T(1,128)S(1)} %get-tuple-element.44), channel_id=1, source_target_pairs={{0,2},{2,4},{4,6},{6,8},{8,10},{10,12},{12,14},{14,16},{16,18},{18... | collective-permute-start | bytes 196616 | tf_op jit(solution)/shard_map/ppermute | solution.py:23
  983.0 6.0 collective-permute-start.28
  984.3 5.0 collective-permute-start.29
  989.3 179.5 %copy-start.6 = (f32[1,32,8,256]{3,2,1,0:T(8,128)S(1)}, f32[1,32,8,256]{3,2,1,0:T(8,128)}, u32[]{:S(2)}) copy-start(f32[1,32,8,256]{3,2,1,0:T(8,128)} %copy-done.5) | copy-start | bytes 786436
  989.3 13.8 collective-permute-start.30
  995.0 8.2 collective-permute-start.31
  996.3 178.1 %collective-permute-start.34 = (f32[2,1,10,256]{3,2,1,0:T(8,128)S(1)}, f32[2,1,10,256]{3,2,1,0:T(8,128)S(1)}, u32[]{:S(2)}, u32[]{:S(2)}) collective-permute-start(f32[2,1,10,256]{3,2,1,0:T(8,128)S(1)} %get-tuple-element.37), channel_id=1, source_target_pairs={{0,1},{2,3},{4,5},{6,7},{8,9},{10,11},{12,13},{14,15},{16,17},{18,... | collective-permute-start | bytes 61448 | tf_op jit(solution)/shard_map/ppermute | solution.py:23
  1001.8 172.7 %collective-permute-start.35 = (f32[2,1,10,256]{3,2,1,0:T(8,128)S(1)}, f32[2,1,10,256]{3,2,1,0:T(8,128)S(1)}, u32[]{:S(2)}, u32[]{:S(2)}) collective-permute-start(f32[2,1,10,256]{3,2,1,0:T(8,128)S(1)} %get-tuple-element.36), channel_id=1, source_target_pairs={{1,0},{3,2},{5,4},{7,6},{9,8},{11,10},{13,12},{15,14},{17,16},{19,... | collective-permute-start | bytes 61448 | tf_op jit(solution)/shard_map/ppermute | solution.py:25
  1169.0 6.5 collective-permute-start.36
  1170.4 5.1 collective-permute-start.37
  1175.5 4.3 collective-permute-start.38
  1176.9 6.1 collective-permute-start.39
  (23 other events, 293.3 us)
Sparse Core Ops, SparseCore 0:
  1193.1 242.0 reduce-scatter.3
